TPU v7x, 128 devices: a whole 4x4x4 slice. The times are simulated.
128 devices in a mesh: group: 4 (over x), tile: 32 (over z, y, core).
Axes of the slice: x: 4, y: 4, z: 4, core: 2. Of those that a mesh axis runs over, the one named last changes fastest.
Arguments:
- frames: bfloat16 [12, 8, 128, 96, 256], P('group', None, 'tile'), may hold values from -6 to 6
- packing: int32 [12, 4], replicated, as said below
- w_space: bfloat16 [3, 3, 96, 96], replicated, may hold values from -0.21875 to 0.21875
- w_time: bfloat16 [3, 96, 96], replicated, may hold values from -0.375 to 0.375
- gain_one: float32 [96], replicated, may hold values from 0.1 to 1.9
- gain_two: float32 [96], replicated, may hold values from 0.1 to 1.9
Outputs:
- output: bfloat16 [12, 8, 128, 96, 256], P('group', None, 'tile')
Inputs may be any that keep to these rules, and one draw needn't show every extreme that they name: `packing`: column 0 is 1 where the slot's span continues a clip and 0 for a clip's first span, whose other source fields are not read. `packing`: a span with a successor has 8 valid frames, so every preceding span is full; the slots of one device have their preceding spans on distinct devices.
All inputs are finite; a program needn't handle non-finite values.
Results may differ from a plain program's by a relative error of at most 0.004.
Values may be sent and summed in bfloat16 or wider, within the bound.
No kernel may reach another device: no remote copies, remote signals or barrier semaphores. Data moves between devices by JAX's collectives and lax.ppermute only.
A program may use at most 192 MiB of HBM per device.

v0:
```python
import jax
import jax.numpy as jnp
from jax import lax
from jax.sharding import PartitionSpec as P


def extended_2(block, sides, width):
    for axis, dim in sides:
        count = lax.axis_size(axis)
        forward = [(i, i + 1) for i in range(count - 1)]
        backward = [(target, source) for source, target in forward]
        low = lax.ppermute(
            lax.slice_in_dim(block, block.shape[dim] - width, None, axis=dim), axis, forward
        )
        high = lax.ppermute(lax.slice_in_dim(block, 0, width, axis=dim), axis, backward)
        block = jnp.concatenate([low, block, high], axis=dim)
    return block


def norm_act(values, gain_vec):
    meansq = jnp.mean(values * values, axis=-2, keepdims=True)
    return jax.nn.silu(values * lax.rsqrt(meansq + 1e-06) * gain_vec[:, None])


def body(frames, packing, w_space, w_time, gain_one, gain_two):
    slot_count, frame_count, row_count, chan_count, col_count = frames.shape
    own_index = lax.axis_index("group")
    mine = lax.dynamic_slice_in_dim(packing, own_index * slot_count, slot_count, 0)
    hidden = norm_act(frames.astype(jnp.float32), gain_one).astype(jnp.bfloat16)
    rimmed = extended_2(hidden, (("tile", 2),), 1)
    padded = jnp.pad(rimmed, ((0, 0), (0, 0), (0, 0), (0, 0), (1, 1)))
    summed = jnp.zeros(frames.shape, jnp.float32)
    for tap_row in range(3):
        for tap_col in range(3):
            window = padded[:, :, tap_row : tap_row + row_count, :, tap_col : tap_col + col_count]
            summed = summed + jnp.einsum(
                "oi,nfyix->nfyox",
                w_space[tap_row, tap_col],
                window,
                preferred_element_type=jnp.float32,
            )
    act = norm_act(summed, gain_two).astype(jnp.bfloat16)
    tails = act[:, frame_count - 2 :]
    has_prev = mine[:, 0] > 0
    wanted = mine[:, 2] * slot_count + mine[:, 3]
    piece = lax.all_gather(tails, "group", axis=0, tiled=True)
    global_ids = jnp.arange(piece.shape[0], dtype=jnp.int32)
    select = ((wanted[:, None] == global_ids[None, :]) & has_prev[:, None]).astype(jnp.bfloat16)
    picked = jnp.einsum("sk,kfyix->sfyix", select, piece, preferred_element_type=jnp.float32)
    cache = picked.astype(jnp.bfloat16)
    extended = jnp.concatenate([cache, act], axis=1)
    temporal = jnp.zeros(frames.shape, jnp.float32)
    for tap in range(3):
        temporal = temporal + jnp.einsum(
            "oi,nfyix->nfyox",
            w_time[tap],
            extended[:, tap : tap + frame_count],
            preferred_element_type=jnp.float32,
        )
    keep = jnp.arange(frame_count, dtype=jnp.int32)[None, :] < mine[:, 1][:, None]
    result = jnp.where(keep[:, :, None, None, None], frames.astype(jnp.float32) + temporal, 0.0)
    return result.astype(jnp.bfloat16)


def solution(mesh):
    in_specs = (P("group", None, "tile", None, None), P(), P(), P(), P(), P())
    out_specs = P("group", None, "tile", None, None)
    return jax.shard_map(body, mesh=mesh, in_specs=in_specs, out_specs=out_specs, check_vma=False)
```

profile of v0, /device:TPU:1, one launch (start us, length us, event | category | flops | bytes accessed | tf_op | source)
XLA Modules:
  0.0 205.3 jit_solution(2057114716746689768)
XLA Ops:
  6.5 3.9 %fusion.6 = f32[3,8,4,256]{3,2,1,0:T(4,128)S(1)} fusion(bf16[3,8,4,96,256]{4,3,2,1,0:T(8,128)(2,1)} %param.6), kind=kLoop, calls=%fused_computation.11 | loop fusion | flops 7053312 | bytes 4816896 | tf_op jit(solution)/shard_map/reduce_sum | solution.py:21
  10.5 4.8 %fusion.13 = bf16[3,8,4,96,256]{4,3,2,1,0:T(8,128)(2,1)S(1)} fusion(bf16[3,8,4,96,256]{4,3,2,1,0:T(8,128)(2,1)} %param.6, f32[96]{0:T(128)} %param.10, f32[3,8,4,256]{3,2,1,0:T(4,128)S(1)} %add_rsqrt_fusion.1), kind=kLoop, calls=%fused_computation.18 | loop fusion | flops 18874368 | bytes 9535872 | tf_op jit(solution)/shard_map/convert_element_type | solution.py:29
  15.5 4.6 %collective-permute-start = (bf16[3,8,1,96,256]{4,3,2,1,0:T(8,128)(2,1)S(1)}, bf16[3,8,1,96,256]{4,3,2,1,0:T(8,128)(2,1)S(1)}, u32[]{:S(2)}, u32[]{:S(2)}) collective-permute-start(bf16[3,8,1,96,256]{4,3,2,1,0:T(8,128)(2,1)S(1)} %get-tuple-element.5), channel_id=1, source_target_pairs={{0,1},{1,2},{2,3},{3,4},{4,5},{5,6},{6,7},{7,8},{8,9},{9,10},{10,1... | collective-permute-start | bytes 3538952 | tf_op jit(solution)/shard_map/ppermute | solution.py:12
  20.1 2.1 %collective-permute-start.1 = (bf16[3,8,1,96,256]{4,3,2,1,0:T(8,128)(2,1)S(1)}, bf16[3,8,1,96,256]{4,3,2,1,0:T(8,128)(2,1)S(1)}, u32[]{:S(2)}, u32[]{:S(2)}) collective-permute-start(bf16[3,8,1,96,256]{4,3,2,1,0:T(8,128)(2,1)S(1)} %get-tuple-element.6), channel_id=1, source_target_pairs={{1,0},{2,1},{3,2},{4,3},{5,4},{6,5},{7,6},{8,7},{9,8},{10,9},{11,1... | collective-permute-start | bytes 3538952 | tf_op jit(solution)/shard_map/ppermute | solution.py:15
  22.2 5.0 %fusion.53 = f32[3,8,4,256,96]{3,4,2,1,0:T(8,128)} fusion(bf16[3,8,4,96,256]{4,3,2,1,0:T(8,128)(2,1)S(1)} %fusion.13, bf16[3,3,96,96]{3,2,1,0:T(8,128)(2,1)S(1)} %copy-done.3), kind=kOutput, calls=%fused_computation.67 | convolution fusion | flops 452984832 | bytes 14180352 | tf_op jit(solution)/shard_map/oi,nfyix->nfyox/dot_general | solution.py:36
  27.3 6.0 %collective-permute-done = bf16[3,8,1,96,256]{4,3,2,1,0:T(8,128)(2,1)S(1)} collective-permute-done((bf16[3,8,1,96,256]{4,3,2,1,0:T(8,128)(2,1)S(1)}, bf16[3,8,1,96,256]{4,3,2,1,0:T(8,128)(2,1)S(1)}, u32[]{:S(2)}, u32[]{:S(2)}) %collective-permute-start) | collective-permute-done | bytes 1179680 | tf_op jit(solution)/shard_map/ppermute | solution.py:12
  33.2 4.4 %collective-permute-done.1 = bf16[3,8,1,96,256]{4,3,2,1,0:T(8,128)(2,1)S(1)} collective-permute-done((bf16[3,8,1,96,256]{4,3,2,1,0:T(8,128)(2,1)S(1)}, bf16[3,8,1,96,256]{4,3,2,1,0:T(8,128)(2,1)S(1)}, u32[]{:S(2)}, u32[]{:S(2)}) %collective-permute-start.1) | collective-permute-done | bytes 1179680 | tf_op jit(solution)/shard_map/ppermute | solution.py:15
  37.6 7.1 %fusion.5 = bf16[3,8,6,96,258]{4,3,2,1,0:T(8,128)(2,1)S(1)} fusion(bf16[3,8,1,96,256]{4,3,2,1,0:T(8,128)(2,1)S(1)} %collective-permute-done.1, bf16[3,8,4,96,256]{4,3,2,1,0:T(8,128)(2,1)S(1)} %fusion.13, bf16[3,8,1,96,256]{4,3,2,1,0:T(8,128)(2,1)S(1)} %collective-permute-done), kind=kLoop, calls=%fused_computation.10 | loop fusion | flops 42799104 | bytes 14211072 | tf_op jit(solution)/shard_map/concatenate | solution.py:16
  44.7 5.5 %fusion.31 = f32[3,8,4,256,96]{3,4,2,1,0:T(8,128)} fusion(bf16[3,8,6,96,258]{4,3,2,1,0:T(8,128)(2,1)S(1)} %fusion.5, bf16[3,3,96,96]{3,2,1,0:T(8,128)(2,1)S(1)} %copy-done.3), kind=kOutput, calls=%fused_computation.43 | convolution fusion | flops 452984832 | bytes 14180352 | tf_op jit(solution)/shard_map/oi,nfyix->nfyox/dot_general | solution.py:36
  50.2 5.2 %fusion.33 = f32[3,8,4,256,96]{3,4,2,1,0:T(8,128)} fusion(bf16[3,8,6,96,258]{4,3,2,1,0:T(8,128)(2,1)S(1)} %fusion.5, bf16[3,3,96,96]{3,2,1,0:T(8,128)(2,1)S(1)} %copy-done.3), kind=kOutput, calls=%fused_computation.45 | convolution fusion | flops 452984832 | bytes 14180352 | tf_op jit(solution)/shard_map/oi,nfyix->nfyox/dot_general | solution.py:36
  55.3 5.1 %fusion.35 = f32[3,8,4,256,96]{3,4,2,1,0:T(8,128)} fusion(bf16[3,8,6,96,258]{4,3,2,1,0:T(8,128)(2,1)S(1)} %fusion.5, bf16[3,3,96,96]{3,2,1,0:T(8,128)(2,1)S(1)} %copy-done.3), kind=kOutput, calls=%fused_computation.47 | convolution fusion | flops 452984832 | bytes 14180352 | tf_op jit(solution)/shard_map/oi,nfyix->nfyox/dot_general | solution.py:36
  60.4 5.1 %fusion.37 = f32[3,8,4,256,96]{3,4,2,1,0:T(8,128)} fusion(bf16[3,8,6,96,258]{4,3,2,1,0:T(8,128)(2,1)S(1)} %fusion.5, bf16[3,3,96,96]{3,2,1,0:T(8,128)(2,1)S(1)} %copy-done.3), kind=kOutput, calls=%fused_computation.49 | convolution fusion | flops 452984832 | bytes 14180352 | tf_op jit(solution)/shard_map/oi,nfyix->nfyox/dot_general | solution.py:36
  65.5 4.9 %fusion.41 = f32[3,8,4,256,96]{3,4,2,1,0:T(8,128)} fusion(bf16[3,8,6,96,258]{4,3,2,1,0:T(8,128)(2,1)S(1)} %fusion.5, bf16[3,3,96,96]{3,2,1,0:T(8,128)(2,1)S(1)} %copy-done.3), kind=kOutput, calls=%fused_computation.54 | convolution fusion | flops 452984832 | bytes 14180352 | tf_op jit(solution)/shard_map/oi,nfyix->nfyox/dot_general | solution.py:36
  70.5 5.1 %fusion.29 = f32[3,8,4,256,96]{3,4,2,1,0:T(8,128)} fusion(bf16[3,8,1,96,256]{4,3,2,1,0:T(8,128)(2,1)S(1)} %collective-permute-done.1, bf16[3,8,4,96,256]{4,3,2,1,0:T(8,128)(2,1)S(1)} %fusion.13, bf16[3,3,96,96]{3,2,1,0:T(8,128)(2,1)S(1)} %copy-done.3), kind=kOutput, calls=%fused_computation.41 | convolution fusion | flops 462422016 | bytes 15360000 | tf_op jit(solution)/shard_map/oi,nfyix->nfyox/dot_general | solution.py:36
  75.6 4.4 %fusion.39 = f32[3,8,4,256,96]{3,4,2,1,0:T(8,128)} fusion(bf16[3,8,4,96,256]{4,3,2,1,0:T(8,128)(2,1)S(1)} %fusion.13, bf16[3,8,1,96,256]{4,3,2,1,0:T(8,128)(2,1)S(1)} %collective-permute-done, bf16[3,3,96,96]{3,2,1,0:T(8,128)(2,1)S(1)} %copy-done.3), kind=kOutput, calls=%fused_computation.52 | convolution fusion | flops 462422016 | bytes 15360000 | tf_op jit(solution)/shard_map/oi,nfyix->nfyox/dot_general | solution.py:36
  80.0 31.7 %multiply_reduce_fusion = (f32[3,8,4,256]{3,2,1,0:T(4,128)S(1)}, f32[3,8,4,256,96]{3,4,2,1,0:T(8,128)}) fusion(bf16[3,8,6,96,258]{4,3,2,1,0:T(8,128)(2,1)} %copy-done.1, bf16[3,3,96,96]{3,2,1,0:T(8,128)(2,1)S(1)} %copy-done.3, f32[3,8,4,256,96]{3,4,2,1,0:T(8,128)} %fusion.29, f32[3,8,4,256,96]{3,4,2,1,0:T(8,128)} %fusion.31, ...), kind=kOutput, calls=%fused_computation.26 | convolution fusion | flops 476553216 | bytes 89776128 | tf_op jit(solution)/shard_map/oi,nfyix->nfyox/dot_general | solution.py:36
  111.8 5.8 %fusion.19 = bf16[3,8,4,96,256]{4,3,2,1,0:T(8,128)(2,1)S(1)} fusion(f32[3,8,4,256,96]{3,4,2,1,0:T(8,128)} %get-tuple-element.10, f32[96]{0:T(128)S(1)} %copy-done.5, f32[3,8,4,256]{3,2,1,0:T(4,128)S(1)} %add_rsqrt_fusion), kind=kLoop, calls=%fused_computation.28 | loop fusion | flops 16515072 | bytes 14254464 | tf_op jit(solution)/shard_map/convert_element_type | solution.py:42
  117.6 2.2 %copy-done.2 = bf16[3,8,4,96,256]{4,3,2,1,0:T(8,128)(2,1)} copy-done((bf16[3,8,4,96,256]{4,3,2,1,0:T(8,128)(2,1)}, bf16[3,8,4,96,256]{4,3,2,1,0:T(8,128)(2,1)S(1)}, u32[]{:S(2)}) %copy-start.2) | copy-done | bytes 4718616
  119.7 1.1 slice.133
  121.0 7.4 %fusion.45 = f32[3,8,4,256,96]{3,4,2,1,0:T(8,128)} fusion(bf16[3,8,4,96,256]{4,3,2,1,0:T(8,128)(2,1)} %copy-done.2, bf16[3,96,96]{2,1,0:T(8,128)(2,1)S(1)} %copy-done.4), kind=kOutput, calls=%fused_computation.59 | convolution fusion | flops 452984832 | bytes 14180352 | tf_op jit(solution)/shard_map/oi,nfyix->nfyox/dot_general | solution.py:54
  128.4 48.3 %all-gather.2.cloned.1.call-done = bf16[12,2,4,96,256]{4,3,2,1,0:T(8,128)(2,1)} async-done(((bf16[3,2,4,96,256]{4,3,2,1,0:T(8,128)(2,1)}), bf16[12,2,4,96,256]{4,3,2,1,0:T(8,128)(2,1)}) %all-gather.2.cloned.1.call-update) | async-done | bytes 4718608 | tf_op jit(solution)/shard_map/all_gather | solution.py:46
  176.7 5.4 %fusion.20 = bf16[3,2,4,96,256]{4,0,3,2,1:T(4,128)(2,1)S(1)} fusion(bf16[12,2,4,96,256]{4,3,2,1,0:T(8,128)(2,1)} %all-gather.2.cloned.1.call-done, s32[3]{0:T(128)S(1)} %get-tuple-element.8, pred[3]{0:T(512)(128)(4,1)S(1)} %compare_bitcast_fusion), kind=kOutput, calls=%fused_computation.29 | convolution fusion | flops 14155848 | bytes 5898255 | tf_op jit(solution)/shard_map/sk,kfyix->sfyix/dot_general | solution.py:49
  182.4 4.4 %fusion.23 = f32[3,8,4,256,96]{3,4,2,1,0:T(8,128)} fusion(bf16[3,2,4,96,256]{4,3,2,1,0:T(8,128)(2,1)S(1)} %copy.27, bf16[3,8,4,96,256]{4,3,2,1,0:T(8,128)(2,1)S(1)} %bitcast.115, bf16[3,96,96]{2,1,0:T(8,128)(2,1)S(1)} %copy-done.4), kind=kOutput, calls=%fused_computation.34 | convolution fusion | flops 462422016 | bytes 15360000 | tf_op jit(solution)/shard_map/oi,nfyix->nfyox/dot_general | solution.py:54
  186.8 11.7 %fusion.15 = bf16[3,8,4,96,256]{4,3,2,1,0:T(8,128)(2,1)} fusion(bf16[3,8,4,96,256]{4,3,2,1,0:T(8,128)(2,1)} %param.6, f32[3,8,4,256,96]{3,4,2,1,0:T(8,128)} %fusion.45, f32[3,8,4,256,96]{3,4,2,1,0:T(8,128)} %fusion.23, pred[3,8]{1,0:T(4,128)(4,1)S(1)} %iota_compare_fusion.3, bf16[3,8,4,96,256]{4,3,2,1,0:T(8,128)(2,1)S(1)} %bitcast.115, ...), kind=kOutput, calls=%fused_computation.20 | convolution fusion | flops 476577792 | bytes 34234880 | tf_op jit(solution)/shard_map/oi,nfyix->nfyox/dot_general | solution.py:54
  (26 shorter events, 0.7 us)
Async XLA Ops:
  6.5 114.3 %copy-start = (s32[12,4]{0,1:T(4,128)S(1)}, s32[12,4]{0,1:T(4,128)}, u32[]{:S(2)}) copy-start(s32[12,4]{0,1:T(4,128)} %param.7) | copy-start | bytes 580
  6.5 15.7 %copy-start.3 = (bf16[3,3,96,96]{3,2,1,0:T(8,128)(2,1)S(1)}, bf16[3,3,96,96]{3,2,1,0:T(8,128)(2,1)}, u32[]{:S(2)}) copy-start(bf16[3,3,96,96]{3,2,1,0:T(8,128)(2,1)} %param.8) | copy-start | bytes 497668
  6.5 170.2 %all-gather.2.cloned.1.call-start = ((), (), s32[]{:S(2)}) async-start(), calls=%async_computation | async-start | bytes 5898240 | tf_op jit(solution)/shard_map/all_gather | solution.py:46
  15.5 17.7 %collective-permute-start = (bf16[3,8,1,96,256]{4,3,2,1,0:T(8,128)(2,1)S(1)}, bf16[3,8,1,96,256]{4,3,2,1,0:T(8,128)(2,1)S(1)}, u32[]{:S(2)}, u32[]{:S(2)}) collective-permute-start(bf16[3,8,1,96,256]{4,3,2,1,0:T(8,128)(2,1)S(1)} %get-tuple-element.5), channel_id=1, source_target_pairs={{0,1},{1,2},{2,3},{3,4},{4,5},{5,6},{6,7},{7,8},{8,9},{9,10},{10,1... | collective-permute-start | bytes 3538952 | tf_op jit(solution)/shard_map/ppermute | solution.py:12
  20.1 17.5 %collective-permute-start.1 = (bf16[3,8,1,96,256]{4,3,2,1,0:T(8,128)(2,1)S(1)}, bf16[3,8,1,96,256]{4,3,2,1,0:T(8,128)(2,1)S(1)}, u32[]{:S(2)}, u32[]{:S(2)}) collective-permute-start(bf16[3,8,1,96,256]{4,3,2,1,0:T(8,128)(2,1)S(1)} %get-tuple-element.6), channel_id=1, source_target_pairs={{1,0},{2,1},{3,2},{4,3},{5,4},{6,5},{7,6},{8,7},{9,8},{10,9},{11,1... | collective-permute-start | bytes 3538952 | tf_op jit(solution)/shard_map/ppermute | solution.py:15
  44.7 20.8 %copy-start.1 = (bf16[3,8,6,96,258]{4,3,2,1,0:T(8,128)(2,1)}, bf16[3,8,6,96,258]{4,3,2,1,0:T(8,128)(2,1)S(1)}, u32[]{:S(2)}) copy-start(bf16[3,8,6,96,258]{4,3,2,1,0:T(8,128)(2,1)S(1)} %fusion.5) | copy-start | bytes 21399556
  80.0 31.8 %copy-start.5 = (f32[96]{0:T(128)S(1)}, f32[96]{0:T(128)}, u32[]{:S(2)}) copy-start(f32[96]{0:T(128)} %param.11) | copy-start | bytes 1156
  111.7 9.4 %copy-start.4 = (bf16[3,96,96]{2,1,0:T(8,128)(2,1)S(1)}, bf16[3,96,96]{2,1,0:T(8,128)(2,1)}, u32[]{:S(2)}) copy-start(bf16[3,96,96]{2,1,0:T(8,128)(2,1)} %param.9) | copy-start | bytes 165892
  117.6 2.2 %copy-start.2 = (bf16[3,8,4,96,256]{4,3,2,1,0:T(8,128)(2,1)}, bf16[3,8,4,96,256]{4,3,2,1,0:T(8,128)(2,1)S(1)}, u32[]{:S(2)}) copy-start(bf16[3,8,4,96,256]{4,3,2,1,0:T(8,128)(2,1)S(1)} %fusion.19) | copy-start | bytes 14155780
  128.4 53.9 %slice-start = ((s8[4718592]{0:T(1024)(128)(4,1)}), s8[524288]{0:T(1024)(128)(4,1)S(1)}, s32[]{:S(2)}) async-start(s8[4718592]{0:T(1024)(128)(4,1)} %bitcast.114), calls=%async_computation.1 | async-start | bytes 1048576
  176.7 5.6 %slice-start.1 = ((s8[4718592]{0:T(1024)(128)(4,1)}), s8[4194304]{0:T(1024)(128)(4,1)S(1)}, s32[]{:S(2)}) async-start(s8[4718592]{0:T(1024)(128)(4,1)} %bitcast.114), calls=%async_computation.2 | async-start | bytes 8388608
Sparse Core Ops, SparseCore 0:
  121.0 55.6 all-gather.1
where the time goes:
time: 205 us
  matrix products  101 us (49%)
  waiting for transfers between devices  58.7 us (29%)
  other arithmetic  21.8 us (11%)
  between operations  13.6 us (7%)
  starting transfers between devices  6.69 us (3%)
  local copies, waits for them, and re-layouts  3.75 us (2%)
    dot_general x9, matrix products, body(): jnp.einsum('oi,nfyix->nfyox', w_space[tap_row, tap_col], window, preferre...  72 us
    all_gather x1, waiting for transfers between devices, body(): piece = lax.all_gather(tails, 'group', axis=0, tiled=True)  48.3 us
    dot_general x3, matrix products, body(): jnp.einsum('oi,nfyix->nfyox', w_time[tap], extended[:, tap:tap + frame_co...  23.5 us
    concatenate x1, other arithmetic, extended_2(): block = jnp.concatenate([low, block, high], axis=dim)  7.08 us
    ppermute x1, waiting for transfers between devices, extended_2(): lax.ppermute(lax.slice_in_dim(block, block.shape[dim] - width, None, axis...  5.96 us
    convert_element_type x1, other arithmetic, body(): act = norm_act(summed, gain_two).astype(jnp.bfloat16)  5.78 us
    dot_general x1, matrix products, body(): jnp.einsum('sk,kfyix->sfyix', select, piece, preferred_element_type=jnp.f...  5.4 us
    convert_element_type x1, other arithmetic, body(): hidden = norm_act(frames.astype(jnp.float32), gain_one).astype(jnp.bfloat16)  4.83 us
  transfers between devices with their start and end apart: 3, of which 3 were waited for; matrix products, arithmetic and copies ran while one was open for 6% of the time, Pallas kernels for 0%

commit v1 on v0

--- a/solution.py
+++ b/solution.py
@@ -43,7 +43,12 @@
     tails = act[:, frame_count - 2 :]
     has_prev = mine[:, 0] > 0
     wanted = mine[:, 2] * slot_count + mine[:, 3]
-    piece = lax.all_gather(tails, "group", axis=0, tiled=True)
+    queue = []
+    for _ in range(jax.lax.psum(1, "group")):
+        queue.append(tails)
+    part_next = jnp.stack(queue, axis=0)
+    x_next = jax.lax.all_to_all(part_next, "group", 0, 0)
+    piece = jnp.concatenate(x_next, 0)
     global_ids = jnp.arange(piece.shape[0], dtype=jnp.int32)
     select = ((wanted[:, None] == global_ids[None, :]) & has_prev[:, None]).astype(jnp.bfloat16)
     picked = jnp.einsum("sk,kfyix->sfyix", select, piece, preferred_element_type=jnp.float32)

time: 205 us -> 197 us (0.961)
  the two profiles are of different devices: /device:TPU:1 before, /device:TPU:64 now
where the time goes in v1:
time: 197 us
  matrix products  101 us (51%)
  waiting for transfers between devices  55.6 us (28%)
  other arithmetic  21.8 us (11%)
  starting transfers between devices  12.8 us (6%)
  local copies, waits for them, and re-layouts  5.46 us (3%)
    dot_general x9, matrix products, body(): jnp.einsum('oi,nfyix->nfyox', w_space[tap_row, tap_col], window, preferre...  71.9 us
    all_to_all x1, waiting for transfers between devices, body(): x_next = jax.lax.all_to_all(part_next, 'group', 0, 0)  47.1 us
    dot_general x3, matrix products, body(): jnp.einsum('oi,nfyix->nfyox', w_time[tap], extended[:, tap:tap + frame_co...  23.5 us
    concatenate x1, other arithmetic, extended_2(): block = jnp.concatenate([low, block, high], axis=dim)  7.08 us
    ppermute x1, waiting for transfers between devices, extended_2(): lax.ppermute(lax.slice_in_dim(block, block.shape[dim] - width, None, axis...  6.7 us
    ppermute x1, starting transfers between devices, extended_2(): lax.ppermute(lax.slice_in_dim(block, 0, width, axis=dim), axis, backward)  5.93 us
    convert_element_type x1, other arithmetic, body(): act = norm_act(summed, gain_two).astype(jnp.bfloat16)  5.78 us
    dot_general x1, matrix products, body(): jnp.einsum('sk,kfyix->sfyix', select, piece, preferred_element_type=jnp.f...  5.4 us
  transfers between devices with their start and end apart: 3, of which 3 were waited for; matrix products, arithmetic and copies ran while one was open for 6% of the time, Pallas kernels for 0%

profile of v1, /device:TPU:64, one launch (start us, length us, event | category | flops | bytes accessed | tf_op | source)
XLA Modules:
  0.0 196.6 jit_solution(12665773499144607125)
XLA Ops:
  0.0 3.9 %fusion.6 = f32[3,8,4,256]{3,2,1,0:T(4,128)S(1)} fusion(bf16[3,8,4,96,256]{4,3,2,1,0:T(8,128)(2,1)} %param.6), kind=kLoop, calls=%fused_computation.11 | loop fusion | flops 7053312 | bytes 4816896 | tf_op jit(solution)/shard_map/reduce_sum | solution.py:21
  4.0 4.8 %fusion.13 = bf16[3,8,4,96,256]{4,3,2,1,0:T(8,128)(2,1)S(1)} fusion(bf16[3,8,4,96,256]{4,3,2,1,0:T(8,128)(2,1)} %param.6, f32[96]{0:T(128)} %param.10, f32[3,8,4,256]{3,2,1,0:T(4,128)S(1)} %add_rsqrt_fusion.1), kind=kLoop, calls=%fused_computation.18 | loop fusion | flops 18874368 | bytes 9535872 | tf_op jit(solution)/shard_map/convert_element_type | solution.py:29
  9.0 1.9 collective-permute-start
  10.9 5.9 %collective-permute-start.1 = (bf16[3,8,1,96,256]{4,3,2,1,0:T(8,128)(2,1)S(1)}, bf16[3,8,1,96,256]{4,3,2,1,0:T(8,128)(2,1)S(1)}, u32[]{:S(2)}, u32[]{:S(2)}) collective-permute-start(bf16[3,8,1,96,256]{4,3,2,1,0:T(8,128)(2,1)S(1)} %get-tuple-element.6), channel_id=1, source_target_pairs={{1,0},{2,1},{3,2},{4,3},{5,4},{6,5},{7,6},{8,7},{9,8},{10,9},{11,1... | collective-permute-start | bytes 3538952 | tf_op jit(solution)/shard_map/ppermute | solution.py:15
  16.8 5.0 %fusion.53 = f32[3,8,4,256,96]{3,4,2,1,0:T(8,128)} fusion(bf16[3,8,4,96,256]{4,3,2,1,0:T(8,128)(2,1)S(1)} %fusion.13, bf16[3,3,96,96]{3,2,1,0:T(8,128)(2,1)S(1)} %copy-done.3), kind=kOutput, calls=%fused_computation.67 | convolution fusion | flops 452984832 | bytes 14180352 | tf_op jit(solution)/shard_map/oi,nfyix->nfyox/dot_general | solution.py:36
  21.9 6.7 %collective-permute-done = bf16[3,8,1,96,256]{4,3,2,1,0:T(8,128)(2,1)S(1)} collective-permute-done((bf16[3,8,1,96,256]{4,3,2,1,0:T(8,128)(2,1)S(1)}, bf16[3,8,1,96,256]{4,3,2,1,0:T(8,128)(2,1)S(1)}, u32[]{:S(2)}, u32[]{:S(2)}) %collective-permute-start) | collective-permute-done | bytes 1179680 | tf_op jit(solution)/shard_map/ppermute | solution.py:12
  30.4 7.1 %fusion.5 = bf16[3,8,6,96,258]{4,3,2,1,0:T(8,128)(2,1)S(1)} fusion(bf16[3,8,1,96,256]{4,3,2,1,0:T(8,128)(2,1)S(1)} %collective-permute-done.1, bf16[3,8,4,96,256]{4,3,2,1,0:T(8,128)(2,1)S(1)} %fusion.13, bf16[3,8,1,96,256]{4,3,2,1,0:T(8,128)(2,1)S(1)} %collective-permute-done), kind=kLoop, calls=%fused_computation.10 | loop fusion | flops 42799104 | bytes 14211072 | tf_op jit(solution)/shard_map/concatenate | solution.py:16
  37.5 5.4 %fusion.31 = f32[3,8,4,256,96]{3,4,2,1,0:T(8,128)} fusion(bf16[3,8,6,96,258]{4,3,2,1,0:T(8,128)(2,1)S(1)} %fusion.5, bf16[3,3,96,96]{3,2,1,0:T(8,128)(2,1)S(1)} %copy-done.3), kind=kOutput, calls=%fused_computation.43 | convolution fusion | flops 452984832 | bytes 14180352 | tf_op jit(solution)/shard_map/oi,nfyix->nfyox/dot_general | solution.py:36
  42.9 5.2 %fusion.33 = f32[3,8,4,256,96]{3,4,2,1,0:T(8,128)} fusion(bf16[3,8,6,96,258]{4,3,2,1,0:T(8,128)(2,1)S(1)} %fusion.5, bf16[3,3,96,96]{3,2,1,0:T(8,128)(2,1)S(1)} %copy-done.3), kind=kOutput, calls=%fused_computation.45 | convolution fusion | flops 452984832 | bytes 14180352 | tf_op jit(solution)/shard_map/oi,nfyix->nfyox/dot_general | solution.py:36
  48.1 5.1 %fusion.35 = f32[3,8,4,256,96]{3,4,2,1,0:T(8,128)} fusion(bf16[3,8,6,96,258]{4,3,2,1,0:T(8,128)(2,1)S(1)} %fusion.5, bf16[3,3,96,96]{3,2,1,0:T(8,128)(2,1)S(1)} %copy-done.3), kind=kOutput, calls=%fused_computation.47 | convolution fusion | flops 452984832 | bytes 14180352 | tf_op jit(solution)/shard_map/oi,nfyix->nfyox/dot_general | solution.py:36
  53.1 5.1 %fusion.37 = f32[3,8,4,256,96]{3,4,2,1,0:T(8,128)} fusion(bf16[3,8,6,96,258]{4,3,2,1,0:T(8,128)(2,1)S(1)} %fusion.5, bf16[3,3,96,96]{3,2,1,0:T(8,128)(2,1)S(1)} %copy-done.3), kind=kOutput, calls=%fused_computation.49 | convolution fusion | flops 452984832 | bytes 14180352 | tf_op jit(solution)/shard_map/oi,nfyix->nfyox/dot_general | solution.py:36
  58.3 4.9 %fusion.41 = f32[3,8,4,256,96]{3,4,2,1,0:T(8,128)} fusion(bf16[3,8,6,96,258]{4,3,2,1,0:T(8,128)(2,1)S(1)} %fusion.5, bf16[3,3,96,96]{3,2,1,0:T(8,128)(2,1)S(1)} %copy-done.3), kind=kOutput, calls=%fused_computation.54 | convolution fusion | flops 452984832 | bytes 14180352 | tf_op jit(solution)/shard_map/oi,nfyix->nfyox/dot_general | solution.py:36
  63.2 5.1 %fusion.29 = f32[3,8,4,256,96]{3,4,2,1,0:T(8,128)} fusion(bf16[3,8,1,96,256]{4,3,2,1,0:T(8,128)(2,1)S(1)} %collective-permute-done.1, bf16[3,8,4,96,256]{4,3,2,1,0:T(8,128)(2,1)S(1)} %fusion.13, bf16[3,3,96,96]{3,2,1,0:T(8,128)(2,1)S(1)} %copy-done.3), kind=kOutput, calls=%fused_computation.41 | convolution fusion | flops 462422016 | bytes 15360000 | tf_op jit(solution)/shard_map/oi,nfyix->nfyox/dot_general | solution.py:36
  68.3 4.4 %fusion.39 = f32[3,8,4,256,96]{3,4,2,1,0:T(8,128)} fusion(bf16[3,8,4,96,256]{4,3,2,1,0:T(8,128)(2,1)S(1)} %fusion.13, bf16[3,8,1,96,256]{4,3,2,1,0:T(8,128)(2,1)S(1)} %collective-permute-done, bf16[3,3,96,96]{3,2,1,0:T(8,128)(2,1)S(1)} %copy-done.3), kind=kOutput, calls=%fused_computation.52 | convolution fusion | flops 462422016 | bytes 15360000 | tf_op jit(solution)/shard_map/oi,nfyix->nfyox/dot_general | solution.py:36
  72.7 31.6 %multiply_reduce_fusion = (f32[3,8,4,256]{3,2,1,0:T(4,128)S(1)}, f32[3,8,4,256,96]{3,4,2,1,0:T(8,128)}) fusion(bf16[3,8,6,96,258]{4,3,2,1,0:T(8,128)(2,1)} %copy-done.1, bf16[3,3,96,96]{3,2,1,0:T(8,128)(2,1)S(1)} %copy-done.3, f32[3,8,4,256,96]{3,4,2,1,0:T(8,128)} %fusion.29, f32[3,8,4,256,96]{3,4,2,1,0:T(8,128)} %fusion.31, ...), kind=kOutput, calls=%fused_computation.26 | convolution fusion | flops 476553216 | bytes 89776128 | tf_op jit(solution)/shard_map/oi,nfyix->nfyox/dot_general | solution.py:36
  104.4 5.8 %fusion.19 = bf16[3,8,4,96,256]{4,3,2,1,0:T(8,128)(2,1)S(1)} fusion(f32[3,8,4,256,96]{3,4,2,1,0:T(8,128)} %get-tuple-element.10, f32[96]{0:T(128)S(1)} %copy-done.5, f32[3,8,4,256]{3,2,1,0:T(4,128)S(1)} %add_rsqrt_fusion), kind=kLoop, calls=%fused_computation.28 | loop fusion | flops 16515072 | bytes 14254464 | tf_op jit(solution)/shard_map/convert_element_type | solution.py:42
  110.2 2.2 %copy-done.2 = bf16[3,8,4,96,256]{4,3,2,1,0:T(8,128)(2,1)} copy-done((bf16[3,8,4,96,256]{4,3,2,1,0:T(8,128)(2,1)}, bf16[3,8,4,96,256]{4,3,2,1,0:T(8,128)(2,1)S(1)}, u32[]{:S(2)}) %copy-start.2) | copy-done | bytes 4718616
  112.4 2.7 %stack.2 = bf16[4,3,2,4,96,256]{5,4,3,2,1,0:T(8,128)(2,1)} broadcast(bf16[3,2,4,96,256]{4,3,2,1,0:T(8,128)(2,1)S(1)} %slice.133), dimensions={1,2,3,4,5} | broadcast | bytes 5898240 | tf_op jit(solution)/shard_map/stack | solution.py:49
  115.1 4.9 %all-to-all-start = ((bf16[4,3,2,4,96,256]{5,4,3,2,1,0:T(8,128)(2,1)}), bf16[4,3,2,4,96,256]{5,4,3,2,1,0:T(8,128)(2,1)}, u32[]{:S(2)}, u32[]{:S(2)}) async-start(bf16[4,3,2,4,96,256]{5,4,3,2,1,0:T(8,128)(2,1)} %stack.2), calls=%async_computation | async-start | bytes 9437184 | tf_op jit(solution)/shard_map/all_to_all | solution.py:50
  120.3 7.4 %fusion.45 = f32[3,8,4,256,96]{3,4,2,1,0:T(8,128)} fusion(bf16[3,8,4,96,256]{4,3,2,1,0:T(8,128)(2,1)} %copy-done.2, bf16[3,96,96]{2,1,0:T(8,128)(2,1)S(1)} %copy-done.4), kind=kOutput, calls=%fused_computation.59 | convolution fusion | flops 452984832 | bytes 14180352 | tf_op jit(solution)/shard_map/oi,nfyix->nfyox/dot_general | solution.py:59
  127.6 47.1 %all-to-all-done = bf16[4,3,2,4,96,256]{5,4,3,2,1,0:T(8,128)(2,1)} async-done(((bf16[4,3,2,4,96,256]{5,4,3,2,1,0:T(8,128)(2,1)}), bf16[4,3,2,4,96,256]{5,4,3,2,1,0:T(8,128)(2,1)}, u32[]{:S(2)}, u32[]{:S(2)}) %all-to-all-start) | async-done | bytes 4718624 | tf_op jit(solution)/shard_map/all_to_all | solution.py:50
  174.8 5.4 %fusion.20 = bf16[3,2,4,96,256]{4,0,3,2,1:T(4,128)(2,1)S(1)} fusion(bf16[12,2,4,96,256]{4,3,2,1,0:T(8,128)(2,1)} %bitcast.33, s32[3]{0:T(128)S(1)} %get-tuple-element.8, pred[3]{0:T(512)(128)(4,1)S(1)} %compare_bitcast_fusion), kind=kOutput, calls=%fused_computation.29 | convolution fusion | flops 14155848 | bytes 5898255 | tf_op jit(solution)/shard_map/sk,kfyix->sfyix/dot_general | solution.py:54
  180.4 4.4 %fusion.23 = f32[3,8,4,256,96]{3,4,2,1,0:T(8,128)} fusion(bf16[3,2,4,96,256]{4,3,2,1,0:T(8,128)(2,1)S(1)} %copy.27, bf16[3,8,4,96,256]{4,3,2,1,0:T(8,128)(2,1)S(1)} %bitcast.116, bf16[3,96,96]{2,1,0:T(8,128)(2,1)S(1)} %copy-done.4), kind=kOutput, calls=%fused_computation.34 | convolution fusion | flops 462422016 | bytes 15360000 | tf_op jit(solution)/shard_map/oi,nfyix->nfyox/dot_general | solution.py:59
  184.9 11.7 %fusion.15 = bf16[3,8,4,96,256]{4,3,2,1,0:T(8,128)(2,1)} fusion(bf16[3,8,4,96,256]{4,3,2,1,0:T(8,128)(2,1)} %param.6, f32[3,8,4,256,96]{3,4,2,1,0:T(8,128)} %fusion.45, f32[3,8,4,256,96]{3,4,2,1,0:T(8,128)} %fusion.23, pred[3,8]{1,0:T(4,128)(4,1)S(1)} %iota_compare_fusion.3, bf16[3,8,4,96,256]{4,3,2,1,0:T(8,128)(2,1)S(1)} %bitcast.116, ...), kind=kOutput, calls=%fused_computation.20 | convolution fusion | flops 476577792 | bytes 34234880 | tf_op jit(solution)/shard_map/oi,nfyix->nfyox/dot_general | solution.py:59
  (26 shorter events, 2.5 us)
Async XLA Ops:
  0.0 120.1 %copy-start = (s32[12,4]{0,1:T(4,128)S(1)}, s32[12,4]{0,1:T(4,128)}, u32[]{:S(2)}) copy-start(s32[12,4]{0,1:T(4,128)} %param.7) | copy-start | bytes 580
  0.0 16.8 %copy-start.3 = (bf16[3,3,96,96]{3,2,1,0:T(8,128)(2,1)S(1)}, bf16[3,3,96,96]{3,2,1,0:T(8,128)(2,1)}, u32[]{:S(2)}) copy-start(bf16[3,3,96,96]{3,2,1,0:T(8,128)(2,1)} %param.8) | copy-start | bytes 497668
  9.0 19.6 %collective-permute-start = (bf16[3,8,1,96,256]{4,3,2,1,0:T(8,128)(2,1)S(1)}, bf16[3,8,1,96,256]{4,3,2,1,0:T(8,128)(2,1)S(1)}, u32[]{:S(2)}, u32[]{:S(2)}) collective-permute-start(bf16[3,8,1,96,256]{4,3,2,1,0:T(8,128)(2,1)S(1)} %get-tuple-element.5), channel_id=1, source_target_pairs={{0,1},{1,2},{2,3},{3,4},{4,5},{5,6},{6,7},{7,8},{8,9},{9,10},{10,1... | collective-permute-start | bytes 3538952 | tf_op jit(solution)/shard_map/ppermute | solution.py:12
  10.9 19.5 %collective-permute-start.1 = (bf16[3,8,1,96,256]{4,3,2,1,0:T(8,128)(2,1)S(1)}, bf16[3,8,1,96,256]{4,3,2,1,0:T(8,128)(2,1)S(1)}, u32[]{:S(2)}, u32[]{:S(2)}) collective-permute-start(bf16[3,8,1,96,256]{4,3,2,1,0:T(8,128)(2,1)S(1)} %get-tuple-element.6), channel_id=1, source_target_pairs={{1,0},{2,1},{3,2},{4,3},{5,4},{6,5},{7,6},{8,7},{9,8},{10,9},{11,1... | collective-permute-start | bytes 3538952 | tf_op jit(solution)/shard_map/ppermute | solution.py:15
  37.4 20.8 %copy-start.1 = (bf16[3,8,6,96,258]{4,3,2,1,0:T(8,128)(2,1)}, bf16[3,8,6,96,258]{4,3,2,1,0:T(8,128)(2,1)S(1)}, u32[]{:S(2)}) copy-start(bf16[3,8,6,96,258]{4,3,2,1,0:T(8,128)(2,1)S(1)} %fusion.5) | copy-start | bytes 21399556
  72.7 31.6 %copy-start.5 = (f32[96]{0:T(128)S(1)}, f32[96]{0:T(128)}, u32[]{:S(2)}) copy-start(f32[96]{0:T(128)} %param.11) | copy-start | bytes 1156
  110.1 2.2 %copy-start.2 = (bf16[3,8,4,96,256]{4,3,2,1,0:T(8,128)(2,1)}, bf16[3,8,4,96,256]{4,3,2,1,0:T(8,128)(2,1)S(1)}, u32[]{:S(2)}) copy-start(bf16[3,8,4,96,256]{4,3,2,1,0:T(8,128)(2,1)S(1)} %fusion.19) | copy-start | bytes 14155780
  112.3 7.9 %copy-start.4 = (bf16[3,96,96]{2,1,0:T(8,128)(2,1)S(1)}, bf16[3,96,96]{2,1,0:T(8,128)(2,1)}, u32[]{:S(2)}) copy-start(bf16[3,96,96]{2,1,0:T(8,128)(2,1)} %param.9) | copy-start | bytes 165892
  115.1 59.6 %all-to-all-start = ((bf16[4,3,2,4,96,256]{5,4,3,2,1,0:T(8,128)(2,1)}), bf16[4,3,2,4,96,256]{5,4,3,2,1,0:T(8,128)(2,1)}, u32[]{:S(2)}, u32[]{:S(2)}) async-start(bf16[4,3,2,4,96,256]{5,4,3,2,1,0:T(8,128)(2,1)} %stack.2), calls=%async_computation | async-start | bytes 9437184 | tf_op jit(solution)/shard_map/all_to_all | solution.py:50
  127.6 52.8 %slice-start = ((s8[4718592]{0:T(1024)(128)(4,1)}), s8[524288]{0:T(1024)(128)(4,1)S(1)}, s32[]{:S(2)}) async-start(s8[4718592]{0:T(1024)(128)(4,1)} %bitcast.115), calls=%async_computation.1 | async-start | bytes 1048576
  174.8 5.6 %slice-start.1 = ((s8[4718592]{0:T(1024)(128)(4,1)}), s8[4194304]{0:T(1024)(128)(4,1)S(1)}, s32[]{:S(2)}) async-start(s8[4718592]{0:T(1024)(128)(4,1)} %bitcast.115), calls=%async_computation.2 | async-start | bytes 8388608
